TPU v7x, 32 devices: a whole 2x2x4 slice. The times are simulated.
32 devices in a mesh: seq: 4 (over z_hi, core), expert: 4 (over y, x), tensor: 2 (over z_lo).
Axes of the slice: x: 2, y: 2, z: 4 (z_hi: 2, z_lo: 2; z = z_hi * 2 + z_lo), core: 2. Of those that a mesh axis runs over, the one named last changes fastest.
Arguments:
- q_rows: bfloat16 [4, 512, 4096], P('expert', 'seq', 'tensor'), may hold values from -6 to 6
- k_rows: bfloat16 [4, 512, 512], P('expert', 'seq', 'tensor'), may hold values from -6 to 6
- value_rows: bfloat16 [4, 512, 512], P('expert', 'seq', 'tensor'), may hold values from -6 to 6
- x_rows: bfloat16 [4, 512, 2048], P('expert', 'seq'), may hold values from -40 to 40
- out_weight: bfloat16 [4096, 2048], P('tensor', 'expert'), may hold values from -0.09375 to 0.09375
- norm_gain: float32 [2048], P('tensor'), may hold values from 0.1 to 1.9
- w_gate: bfloat16 [16, 2048, 768], P(('seq', 'expert'), None, 'tensor'), may hold values from -0.125 to 0.125
- w_up: bfloat16 [16, 2048, 768], P(('seq', 'expert'), None, 'tensor'), may hold values from -0.125 to 0.125
- w_down: bfloat16 [16, 768, 2048], P(('seq', 'expert'), 'tensor'), may hold values from -0.21875 to 0.21875
- expert_ids: int32 [4, 512, 8], P('expert', 'seq'), may hold values from 0 to 15, all different within a row; in each aligned block of 128 rows (0 to 127, 128 to 255, ..., all dimensions but the last counted through in order) at most 96 rows name the same one
- gate_weights: float32 [4, 512, 8], P('expert', 'seq'), may hold values from 0.02 to 0.4
Outputs:
- layer_out: bfloat16 [4, 512, 2048], P('expert', 'seq', 'tensor')
Inputs may be any that keep to these rules, and one draw needn't show every extreme that they name: `expert_ids`: in each token's row the 8 ids differ. Among the 128 tokens of one block of positions (the blocks laid session after session) no expert is named more than 96 times, a bound that some block reaches; every expert is named somewhere.
All inputs are finite; a program needn't handle non-finite values.
Results may differ from a plain program's by a relative error of at most 0.007.
Values may be sent and summed in bfloat16 or wider, within the bound.
No kernel may reach another device: no remote copies, remote signals or barrier semaphores. Data moves between devices by JAX's collectives and lax.ppermute only.
A program may use at most 128 MiB of HBM per device.

v0:
```python
import math
import jax
import jax.numpy as jnp
from jax import lax
from jax.sharding import PartitionSpec as P

HEAD_SIZE = 128
TOPK = 8


def per_device(
    q_rows,
    k_rows,
    value_rows,
    x_rows,
    out_weight,
    norm_gain,
    w_gate,
    w_up,
    w_down,
    expert_ids,
    gate_weights,
):
    rows_here = q_rows.shape[1]
    kv_heads = k_rows.shape[2] // HEAD_SIZE
    q_heads = q_rows.shape[2] // HEAD_SIZE
    group_width = q_heads // kv_heads
    queries = q_rows[0].reshape(rows_here, kv_heads, group_width, HEAD_SIZE)
    offset = lax.axis_index("seq") * rows_here
    query_pos = offset + jnp.arange(rows_here, dtype=jnp.int32)
    softmax_scale = 1.0 / math.sqrt(HEAD_SIZE)
    tensor_pos = lax.axis_index("tensor")
    tensor_count = lax.axis_size("tensor")
    pieces = (
        lax.all_gather(k_rows, "seq", axis=1, tiled=True),
        lax.all_gather(value_rows, "seq", axis=1, tiled=True),
    )
    running_max = jnp.full((kv_heads, group_width, rows_here), -1e30, jnp.float32)
    block_rows = pieces[0].shape[1]
    key_block = pieces[0][0].reshape(block_rows, kv_heads, HEAD_SIZE)
    value_block = pieces[1][0].reshape(block_rows, kv_heads, HEAD_SIZE)
    scores = (
        jnp.einsum("igrd,jgd->grij", queries, key_block, preferred_element_type=jnp.float32)
        * softmax_scale
    )
    key_pos = jnp.arange(block_rows, dtype=jnp.int32)
    allowed = key_pos[None, :] <= query_pos[:, None]
    scores = jnp.where(allowed, scores, jnp.float32(-1e30))
    new_max = jnp.maximum(running_max, jnp.max(scores, axis=-1))
    weights = jnp.where(allowed, jnp.exp(scores - new_max[..., None]), jnp.float32(0.0))
    running_sum = jnp.sum(weights, axis=-1)
    weighted = jnp.einsum(
        "grij,jgd->grid",
        weights.astype(jnp.bfloat16),
        value_block,
        preferred_element_type=jnp.float32,
    )
    running_max, running_sum, weighted = (new_max, running_sum, weighted)
    attn_rows = (
        (weighted / running_sum[..., None])
        .transpose(2, 0, 1, 3)
        .reshape(rows_here, q_heads * HEAD_SIZE)
        .astype(jnp.bfloat16)
    )
    head_terms = jnp.dot(
        attn_rows,
        lax.all_gather(out_weight, "expert", axis=1, tiled=True),
        preferred_element_type=jnp.float32,
    )
    width = x_rows.shape[2]
    half_width = width // tensor_count
    share_sum = lax.psum_scatter(
        head_terms.astype(jnp.bfloat16), "tensor", scatter_dimension=1, tiled=True
    ).astype(jnp.float32)
    mixed_half = (
        lax.dynamic_slice_in_dim(x_rows[0], tensor_pos * half_width, half_width, 1).astype(
            jnp.float32
        )
        + share_sum
    )
    power = lax.psum(jnp.sum(mixed_half * mixed_half, axis=1), "tensor")
    inverse = lax.rsqrt(power / width + 1e-06)
    normed = (mixed_half * inverse[:, None] * norm_gain[None, :]).astype(jnp.bfloat16)
    seq_count = lax.axis_size("seq")
    group_count = lax.axis_size("expert")
    experts = seq_count * group_count
    capacity = max(2, 3 * rows_here * TOPK // (2 * experts))
    routed = expert_ids[0].reshape(-1)
    assigned = routed.shape[0]
    member = (routed[:, None] == jnp.arange(experts, dtype=jnp.int32)[None, :]).astype(jnp.int32)
    earlier = jnp.cumsum(member, axis=0) - member
    slot_index = jnp.sum(earlier * member, axis=1)
    target = routed * capacity + slot_index
    owner_index = (
        jnp.full((experts * capacity,), assigned, jnp.int32)
        .at[target]
        .set(jnp.arange(assigned, dtype=jnp.int32))
    )
    filled = owner_index < assigned
    source = jnp.minimum(owner_index // TOPK, rows_here - 1)
    outgoing = jnp.where(filled[:, None], normed[source], jnp.zeros((), jnp.bfloat16)).reshape(
        experts, capacity, half_width
    )
    arrived = lax.all_to_all(outgoing, ("seq", "expert"), split_axis=0, concat_axis=0, tiled=True)
    slot_count = arrived.shape[1]
    whole_rows = lax.all_gather(arrived, "tensor", axis=2, tiled=True)
    flat_rows = whole_rows.reshape(-1, whole_rows.shape[2])
    gate_act = jnp.dot(flat_rows, w_gate[0], preferred_element_type=jnp.float32)
    up_act = jnp.dot(flat_rows, w_up[0], preferred_element_type=jnp.float32)
    hidden = (jax.nn.silu(gate_act) * up_act).astype(jnp.bfloat16)
    partial_value = jnp.dot(hidden, w_down[0], preferred_element_type=jnp.float32).reshape(
        arrived.shape[0], slot_count, whole_rows.shape[2]
    )
    returned = lax.all_to_all(
        lax.psum_scatter(
            partial_value.astype(jnp.bfloat16), "tensor", scatter_dimension=2, tiled=True
        ),
        ("seq", "expert"),
        split_axis=0,
        concat_axis=0,
        tiled=True,
    )
    came_back = returned.reshape(experts * capacity, half_width)
    picked = came_back[target].astype(jnp.float32)
    weights_flat = gate_weights[0].reshape(-1)
    blended = jnp.sum((picked * weights_flat[:, None]).reshape(rows_here, TOPK, half_width), axis=1)
    return (mixed_half + blended).astype(jnp.bfloat16)[None]


def solution(mesh):
    return jax.shard_map(
        per_device,
        mesh=mesh,
        in_specs=(
            P("expert", "seq", "tensor"),
            P("expert", "seq", "tensor"),
            P("expert", "seq", "tensor"),
            P("expert", "seq", None),
            P("tensor", "expert"),
            P("tensor"),
            P(("seq", "expert"), None, "tensor"),
            P(("seq", "expert"), None, "tensor"),
            P(("seq", "expert"), "tensor", None),
            P("expert", "seq", None),
            P("expert", "seq", None),
        ),
        out_specs=P("expert", "seq", "tensor"),
        check_vma=False,
    )
```

profile of v0, /device:TPU:0, one launch (start us, length us, event | category | flops | bytes accessed | tf_op | source)
XLA Modules:
  0.0 479.6 jit_solution(12763142694707594264)
XLA Ops:
  6.6 0.7 all-gather.3.cloned.1.call-update
  7.3 0.8 copy.24
  8.3 1.1 copy.34
  9.6 9.7 %all_gather.13 = bf16[1,512,256]{2,1,0:T(8,128)(2,1)S(1)} all-gather(bf16[1,128,256]{2,1,0:T(8,128)(2,1)S(1)} %copy-done.3), channel_id=1, replica_groups=mesh['seq'=4,'expert'=4,'tensor'=2] {'seq'}, dimensions={1}, use_global_device_ids=true | all-gather | bytes 327680 | tf_op jit(solution)/shard_map/all_gather | solution.py:36
  19.3 0.1 copy.21
  19.5 4.5 reduce-window.6
  24.1 0.1 copy.26
  24.5 8.2 %all_gather.12 = bf16[1,512,256]{1,2,0:T(8,128)(2,1)S(1)} all-gather(bf16[1,128,256]{1,2,0:T(8,128)(2,1)S(1)} %copy.18), channel_id=1, replica_groups=mesh['seq'=4,'expert'=4,'tensor'=2] {'seq'}, dimensions={1}, use_global_device_ids=true | all-gather | bytes 327680 | tf_op jit(solution)/shard_map/all_gather | solution.py:35
  32.8 0.9 fusion.1
  33.7 1.0 fusion.2
  34.7 1.2 divide_convert_fusion
  35.9 63.4 %all-gather.3.cloned.1.call-done = bf16[2048,2048]{1,0:T(8,128)(2,1)} async-done(((bf16[2048,512]{1,0:T(8,128)(2,1)}), bf16[2048,2048]{1,0:T(8,128)(2,1)}) %all-gather.3.cloned.1.call-update) | async-done | bytes 8388624 | tf_op jit(solution)/shard_map/all_gather | solution.py:67
  99.3 5.6 %convolution_convert_fusion.1 = bf16[128,2048]{1,0:T(8,128)(2,1)} fusion(bf16[128,2048]{0,1:T(8,128)(2,1)S(1)} %bitcast.89, bf16[2048,2048]{1,0:T(8,128)(2,1)} %all-gather.3.cloned.1.call-done), kind=kOutput, calls=%fused_computation.14 | convolution fusion | flops 1074003968 | bytes 9437184 | tf_op jit(solution)/shard_map/dot_general | solution.py:65
  105.1 4.3 scatter_custom_fusion
  109.5 10.1 %reduce-scatter.3.cloned.1.call-done = bf16[128,1024]{1,0:T(8,128)(2,1)} async-done(((bf16[128,2048]{1,0:T(8,128)(2,1)}), bf16[128,1024]{1,0:T(8,128)(2,1)}) %reduce-scatter.3.cloned.1.call-update) | async-done | bytes 262160 | tf_op jit(solution)/shard_map/reduce_scatter | solution.py:72
  119.7 1.1 multiply_reduce_fusion
  120.8 4.9 %psum.7 = f32[128]{0:T(128)S(1)} all-reduce(f32[128]{0:T(128)S(1)} %multiply_reduce_fusion), channel_id=1, replica_groups=mesh['seq'=4,'expert'=4,'tensor'=2] {'tensor'}, use_global_device_ids=true, to_apply=%region_8.9 | all-reduce | flops 128 | bytes 1024 | tf_op jit(solution)/shard_map/psum | solution.py:81
  125.7 1.1 multiply_convert_fusion
  126.8 5.8 %gather_fusion = bf16[1536,1024]{1,0:T(8,128)(2,1)} fusion(bf16[128,1024]{1,0:T(8,128)(2,1)S(1)} %multiply_convert_fusion, s32[2048]{0:T(1024)S(1)} %pad_clamp_fusion), kind=kCustom, calls=%fused_computation | custom fusion | bytes 6297600 | tf_op jit(solution)/shard_map/gather | solution.py:101
  132.6 2.1 broadcast_select_fusion
  134.7 77.7 %all_to_all.10 = bf16[16,96,1024]{2,1,0:T(8,128)(2,1)} all-to-all(bf16[16,96,1024]{2,1,0:T(8,128)(2,1)S(1)} %broadcast_select_fusion), channel_id=1, replica_groups=mesh['seq'=4,'expert'=4,'tensor'=2] {'seq','expert'}, dimensions={0} | all-to-all | bytes 6291456 | tf_op jit(solution)/shard_map/all_to_all | solution.py:104
  212.5 0.2 reduce-scatter.5.cloned.1.call-start
  212.7 77.5 %all-gather.5.cloned.1.call-done = bf16[16,96,2048]{2,1,0:T(8,128)(2,1)} async-done(((bf16[16,96,1024]{2,1,0:T(8,128)(2,1)}), bf16[16,96,2048]{2,1,0:T(8,128)(2,1)}) %all-gather.5.cloned.1.call-update) | async-done | bytes 6291472 | tf_op jit(solution)/shard_map/all_gather | solution.py:106
  290.3 6.1 %fusion.10 = f32[1536,384]{1,0:T(8,128)S(1)} fusion(bf16[1536,2048]{1,0:T(8,128)(2,1)} %bitcast.100, bf16[1,2048,384]{2,1,0:T(8,128)(2,1)} %param.17), kind=kOutput, calls=%fused_computation.19 | convolution fusion | flops 2415919104 | bytes 10223616 | tf_op jit(solution)/shard_map/dot_general | solution.py:108
  296.4 3.9 fusion.4
  300.3 5.4 %convolution_convert_fusion = bf16[16,96,2048]{2,1,0:T(8,128)(2,1)} fusion(bf16[16,96,384]{2,1,0:T(8,128)(2,1)S(1)} %bitcast.102, bf16[1,384,2048]{2,1,0:T(8,128)(2,1)S(1)} %copy-done), kind=kOutput, calls=%fused_computation.3 | convolution fusion | flops 2419064832 | bytes 9043968 | tf_op jit(solution)/shard_map/dot_general | solution.py:111
  305.7 77.3 %reduce-scatter.5.cloned.1.call-done = bf16[16,96,1024]{2,1,0:T(8,128)(2,1)} async-done(((bf16[16,96,2048]{2,1,0:T(8,128)(2,1)}), bf16[16,96,1024]{2,1,0:T(8,128)(2,1)}) %reduce-scatter.5.cloned.1.call-update) | async-done | bytes 3145744 | tf_op jit(solution)/shard_map/reduce_scatter | solution.py:115
  383.0 5.6 %all-to-all-start.1 = ((bf16[16,96,1024]{2,1,0:T(8,128)(2,1)}), bf16[16,96,1024]{2,1,0:T(8,128)(2,1)}, u32[]{:S(2)}, u32[]{:S(2)}) async-start(bf16[16,96,1024]{2,1,0:T(8,128)(2,1)} %reduce-scatter.5.cloned.1.call-done), calls=%async_computation.3 | async-start | bytes 6291456 | tf_op jit(solution)/shard_map/all_to_all | solution.py:114
  388.8 72.2 %all-to-all-done.1 = bf16[16,96,1024]{2,1,0:T(8,128)(2,1)} async-done(((bf16[16,96,1024]{2,1,0:T(8,128)(2,1)}), bf16[16,96,1024]{2,1,0:T(8,128)(2,1)}, u32[]{:S(2)}, u32[]{:S(2)}) %all-to-all-start.1) | async-done | bytes 3145760 | tf_op jit(solution)/shard_map/all_to_all | solution.py:114
  460.9 8.4 %gather_fusion.1 = bf16[1024,1024]{1,0:T(8,128)(2,1)} fusion(bf16[1536,1024]{1,0:T(8,128)(2,1)} %bitcast.21, s32[1024]{0:T(1024)S(1)} %broadcast_clamp_fusion), kind=kCustom, calls=%fused_computation.1 | custom fusion | bytes 4198400 | tf_op jit(solution)/shard_map/gather | solution.py:124
  469.3 2.9 fusion
  472.3 0.8 fusion.19
  (51 shorter events, 1.3 us)
Async XLA Ops:
  6.5 293.7 %copy-start = (bf16[1,384,2048]{2,1,0:T(8,128)(2,1)S(1)}, bf16[1,384,2048]{2,1,0:T(8,128)(2,1)}, u32[]{:S(2)}) copy-start(bf16[1,384,2048]{2,1,0:T(8,128)(2,1)} %param.19) | copy-start | bytes 4718596
  6.5 17.8 %copy-start.5 = (s32[1,128,8]{1,2,0:T(8,128)S(1)}, s32[1,128,8]{1,2,0:T(8,128)}, u32[]{:S(2)}) copy-start(s32[1,128,8]{1,2,0:T(8,128)} %param.20) | copy-start | bytes 12292
  6.5 2.9 copy-start.4
  6.5 3.0 copy-start.3
  6.5 92.7 %all-gather.3.cloned.1.call-start = ((), (), s32[]{:S(2)}) async-start(), calls=%async_computation.4 | async-start | bytes 10485760 | tf_op jit(solution)/shard_map/all_gather | solution.py:67
  7.3 112.4 %reduce-scatter.3.cloned.1.call-start = ((), (), s32[]{:S(2)}) async-start(), calls=%async_computation.5 | async-start | bytes 786432 | tf_op jit(solution)/shard_map/reduce_scatter | solution.py:72
  99.3 20.4 %copy-start.2 = (bf16[1,128,2048]{2,1,0:T(8,128)(2,1)S(1)}, bf16[1,128,2048]{2,1,0:T(8,128)(2,1)}, u32[]{:S(2)}) copy-start(bf16[1,128,2048]{2,1,0:T(8,128)(2,1)} %param.14) | copy-start | bytes 1572868
  99.3 26.4 %copy-start.6 = (f32[1024]{0:T(1024)S(1)}, f32[1024]{0:T(1024)}, u32[]{:S(2)}) copy-start(f32[1024]{0:T(1024)} %param.16) | copy-start | bytes 12292
  104.9 185.4 %all-gather.5.cloned.1.call-start = ((), (), s32[]{:S(2)}) async-start(), calls=%async_computation.6 | async-start | bytes 9437184 | tf_op jit(solution)/shard_map/all_gather | solution.py:106
  212.5 170.5 %reduce-scatter.5.cloned.1.call-start = ((), (), s32[]{:S(2)}) async-start(), calls=%async_computation.7 | async-start | bytes 9437184 | tf_op jit(solution)/shard_map/reduce_scatter | solution.py:115
  290.3 6.1 %copy-start.8 = (bf16[16,96,2048]{2,1,0:T(8,128)(2,1)S(1)}, bf16[16,96,2048]{2,1,0:T(8,128)(2,1)}, u32[]{:S(2)}) copy-start(bf16[16,96,2048]{2,1,0:T(8,128)(2,1)} %all-gather.5.cloned.1.call-done) | copy-start | bytes 18874372
  290.3 6.1 %copy-start.9 = (bf16[1,2048,384]{2,1,0:T(8,128)(2,1)S(1)}, bf16[1,2048,384]{2,1,0:T(8,128)(2,1)}, u32[]{:S(2)}) copy-start(bf16[1,2048,384]{2,1,0:T(8,128)(2,1)} %param.18) | copy-start | bytes 4718596
  305.7 83.0 %copy-start.7 = (f32[1,128,8]{1,2,0:T(8,128)S(1)}, f32[1,128,8]{1,2,0:T(8,128)}, u32[]{:S(2)}) copy-start(f32[1,128,8]{1,2,0:T(8,128)} %param.21) | copy-start | bytes 12292
  383.0 77.9 %all-to-all-start.1 = ((bf16[16,96,1024]{2,1,0:T(8,128)(2,1)}), bf16[16,96,1024]{2,1,0:T(8,128)(2,1)}, u32[]{:S(2)}, u32[]{:S(2)}) async-start(bf16[16,96,1024]{2,1,0:T(8,128)(2,1)} %reduce-scatter.5.cloned.1.call-done), calls=%async_computation.3 | async-start | bytes 6291456 | tf_op jit(solution)/shard_map/all_to_all | solution.py:114
  460.9 11.3 %copy-start.1 = (bf16[128,1024]{1,0:T(8,128)(2,1)S(1)}, bf16[128,1024]{1,0:T(8,128)(2,1)}, u32[]{:S(2)}) copy-start(bf16[128,1024]{1,0:T(8,128)(2,1)} %reduce-scatter.3.cloned.1.call-done) | copy-start | bytes 786436
Sparse Core Ops, SparseCore 0:
  9.2 90.0 all-gather.2
  105.0 14.6 reduce-scatter.2
  212.6 77.5 all-gather.4
  305.8 77.1 reduce-scatter.4
where the time goes:
time: 480 us
  waiting for transfers between devices  301 us (63%)
  blocking collectives  101 us (21%)
  matrix products  23 us (5%)
  local copies, waits for them, and re-layouts  21.6 us (4%)
  other arithmetic  13.8 us (3%)
  between operations  13.4 us (3%)
  starting transfers between devices  5.98 us (1%)
    all_to_all x1, blocking collectives, per_device(): lax.all_to_all(outgoing, ('seq', 'expert'), split_axis=0, concat_axis=0,...  77.7 us
    all_gather x1, waiting for transfers between devices, per_device(): whole_rows = lax.all_gather(arrived, 'tensor', axis=2, tiled=True)  77.5 us
    reduce_scatter x1, waiting for transfers between devices, per_device(): lax.psum_scatter(partial_value.astype(jnp.bfloat16), 'tensor', scatter_di...  77.3 us
    all_to_all x1, waiting for transfers between devices, per_device(): lax.all_to_all(lax.psum_scatter(partial_value.astype(jnp.bfloat16), 'tens...  72.2 us
    all_gather x1, waiting for transfers between devices, per_device(): lax.all_gather(out_weight, 'expert', axis=1, tiled=True)  63.4 us
    reduce_scatter x1, waiting for transfers between devices, per_device(): lax.psum_scatter(head_terms.astype(jnp.bfloat16), 'tensor', scatter_dimen...  10.1 us
    all_gather x1, blocking collectives, per_device(): lax.all_gather(value_rows, 'seq', axis=1, tiled=True)  9.72 us
  transfers between devices with their start and end apart: 5, of which 5 were waited for; matrix products, arithmetic and copies ran while one was open for 3% of the time, Pallas kernels for 0%

commit v1 on v0

--- a/solution.py
+++ b/solution.py
@@ -6,6 +6,27 @@
 
 HEAD_SIZE = 128
 TOPK = 8
+
+
+def gather_around(x, axis, dim):
+    peers, position, rows = (lax.axis_size(axis), lax.axis_index(axis), x.shape[dim])
+    forward = [(i, (i + 1) % peers) for i in range(peers)]
+    left = [(i, (i - 1) % peers) for i in range(peers)]
+    out = jnp.zeros((*x.shape[:dim], peers * rows, *x.shape[dim + 1 :]), x.dtype)
+    out = lax.dynamic_update_slice_in_dim(out, x, position * rows, axis=dim)
+    from_left = from_right = x
+    middle = peers // 2
+    for step in range(1, middle + 1):
+        from_left = lax.ppermute(from_left, axis, forward)
+        out = lax.dynamic_update_slice_in_dim(
+            out, from_left, (position - step) % peers * rows, axis=dim
+        )
+        if step < peers - middle:
+            from_right = lax.ppermute(from_right, axis, left)
+            out = lax.dynamic_update_slice_in_dim(
+                out, from_right, (position + step) % peers * rows, axis=dim
+            )
+    return out
 
 
 def per_device(
@@ -63,9 +84,7 @@
         .astype(jnp.bfloat16)
     )
     head_terms = jnp.dot(
-        attn_rows,
-        lax.all_gather(out_weight, "expert", axis=1, tiled=True),
-        preferred_element_type=jnp.float32,
+        attn_rows, gather_around(out_weight, "expert", 1), preferred_element_type=jnp.float32
     )
     width = x_rows.shape[2]
     half_width = width // tensor_count

time: 480 us -> 526 us (1.096)
  waiting for transfers between devices: 301 us -> 335 us
  local copies, waits for them, and re-layouts: 21.6 us -> 31.3 us
    ppermute x0 -> x3, waiting for transfers between devices: none -> 97.4 us  [the longest x2 74.4 us: gather_around(): from_left = lax.ppermute(from_left, axis, forward)]
    all_gather x1 -> x0, waiting for transfers between devices: 63.4 us -> none  [per_device(): lax.all_gather(out_weight, 'expert', axis=1, tiled=True)]
    dynamic_update_slice x0 -> x4, local copies, waits for them, and re-layouts: none -> 6.06 us  [the longest x2 3.82 us: gather_around(): lax.dynamic_update_slice_in_dim(out, from_left, (position - step) % peers...]
  transfers between devices with their start and end apart: 5 -> 7, of which waited for: 5 -> 7; matrix products, arithmetic and copies ran while one was open for 3% -> 4% of each run, Pallas kernels for 0% -> 0%
where the time goes in v1:
time: 526 us
  waiting for transfers between devices  335 us (64%)
  blocking collectives  99.6 us (19%)
  local copies, waits for them, and re-layouts  31.3 us (6%)
  matrix products  21.5 us (4%)
  other arithmetic  13.8 us (3%)
  between operations  13.4 us (3%)
  starting transfers between devices  11 us (2%)
    all_to_all x1, blocking collectives, per_device(): lax.all_to_all(outgoing, ('seq', 'expert'), split_axis=0, concat_axis=0,...  77.8 us
    all_gather x1, waiting for transfers between devices, per_device(): whole_rows = lax.all_gather(arrived, 'tensor', axis=2, tiled=True)  77.5 us
    reduce_scatter x1, waiting for transfers between devices, per_device(): lax.psum_scatter(partial_value.astype(jnp.bfloat16), 'tensor', scatter_di...  77.3 us
    ppermute x2, waiting for transfers between devices, gather_around(): from_left = lax.ppermute(from_left, axis, forward)  74.4 us
    all_to_all x1, waiting for transfers between devices, per_device(): lax.all_to_all(lax.psum_scatter(partial_value.astype(jnp.bfloat16), 'tens...  72.2 us
    ppermute x1, waiting for transfers between devices, gather_around(): from_right = lax.ppermute(from_right, axis, left)  23 us
    reduce_scatter x1, waiting for transfers between devices, per_device(): lax.psum_scatter(head_terms.astype(jnp.bfloat16), 'tensor', scatter_dimen...  10.7 us
  transfers between devices with their start and end apart: 7, of which 7 were waited for; matrix products, arithmetic and copies ran while one was open for 4% of the time, Pallas kernels for 0%

profile of v1, /device:TPU:0, one launch (start us, length us, event | category | flops | bytes accessed | tf_op | source)
XLA Modules:
  0.0 525.7 jit_solution(17453498298412844224)
XLA Ops:
  6.5 3.0 collective-permute-start
  10.6 1.1 copy.34
  12.7 8.7 %all_gather.9 = bf16[1,512,256]{1,2,0:T(8,128)(2,1)S(1)} all-gather(bf16[1,128,256]{1,2,0:T(8,128)(2,1)S(1)} %copy.18), channel_id=1, replica_groups=mesh['seq'=4,'expert'=4,'tensor'=2] {'seq'}, dimensions={1}, use_global_device_ids=true | all-gather | bytes 327680 | tf_op jit(solution)/shard_map/all_gather | solution.py:56
  21.4 2.8 fusion.1
  24.5 32.8 %collective-permute-done = bf16[2048,512]{1,0:T(8,128)(2,1)} collective-permute-done((bf16[2048,512]{1,0:T(8,128)(2,1)}, bf16[2048,512]{1,0:T(8,128)(2,1)}, u32[]{:S(2)}, u32[]{:S(2)}) %collective-permute-start) | collective-permute-done | bytes 2097184 | tf_op jit(solution)/shard_map/ppermute | solution.py:20
  58.4 8.2 %all_gather.10 = bf16[1,512,256]{2,1,0:T(8,128)(2,1)S(1)} all-gather(bf16[1,128,256]{2,1,0:T(8,128)(2,1)S(1)} %copy-done.5), channel_id=1, replica_groups=mesh['seq'=4,'expert'=4,'tensor'=2] {'seq'}, dimensions={1}, use_global_device_ids=true | all-gather | bytes 327680 | tf_op jit(solution)/shard_map/all_gather | solution.py:57
  66.8 4.5 reduce-window.6
  73.8 1.8 copy-done.1
  76.7 1.2 divide_convert_fusion
  77.9 1.9 constant_dynamic-update-slice_fusion.2
  79.8 23.0 %collective-permute-done.1 = bf16[2048,512]{1,0:T(8,128)(2,1)} collective-permute-done((bf16[2048,512]{1,0:T(8,128)(2,1)}, bf16[2048,512]{1,0:T(8,128)(2,1)}, u32[]{:S(2)}, u32[]{:S(2)}) %collective-permute-start.1) | collective-permute-done | bytes 2097184 | tf_op jit(solution)/shard_map/ppermute | solution.py:25
  102.8 1.9 constant_dynamic-update-slice_fusion.1
  104.7 41.6 %collective-permute-done.2 = bf16[2048,512]{1,0:T(8,128)(2,1)} collective-permute-done((bf16[2048,512]{1,0:T(8,128)(2,1)}, bf16[2048,512]{1,0:T(8,128)(2,1)}, u32[]{:S(2)}, u32[]{:S(2)}) %collective-permute-start.2) | collective-permute-done | bytes 2097184 | tf_op jit(solution)/shard_map/ppermute | solution.py:20
  146.4 1.9 constant_dynamic-update-slice_fusion
  148.3 2.1 convolution_convert_fusion.1
  150.6 4.3 scatter_custom_fusion
  155.1 10.7 %reduce-scatter.3.cloned.1.call-done = bf16[128,1024]{1,0:T(8,128)(2,1)} async-done(((bf16[128,2048]{1,0:T(8,128)(2,1)}), bf16[128,1024]{1,0:T(8,128)(2,1)}) %reduce-scatter.3.cloned.1.call-update) | async-done | bytes 262160 | tf_op jit(solution)/shard_map/reduce_scatter | solution.py:91
  165.8 1.1 multiply_reduce_fusion
  166.9 4.9 psum.7
  171.8 1.1 multiply_convert_fusion
  172.9 5.8 %gather_fusion = bf16[1536,1024]{1,0:T(8,128)(2,1)} fusion(bf16[128,1024]{1,0:T(8,128)(2,1)S(1)} %multiply_convert_fusion, s32[2048]{0:T(1024)S(1)} %pad_clamp_fusion), kind=kCustom, calls=%fused_computation | custom fusion | bytes 6297600 | tf_op jit(solution)/shard_map/gather | solution.py:120
  178.7 2.1 broadcast_select_fusion
  180.8 77.8 %all_to_all.10 = bf16[16,96,1024]{2,1,0:T(8,128)(2,1)} all-to-all(bf16[16,96,1024]{2,1,0:T(8,128)(2,1)S(1)} %broadcast_select_fusion), channel_id=1, replica_groups=mesh['seq'=4,'expert'=4,'tensor'=2] {'seq','expert'}, dimensions={0} | all-to-all | bytes 6291456 | tf_op jit(solution)/shard_map/all_to_all | solution.py:123
  258.8 77.5 %all-gather.2.cloned.1.call-done = bf16[16,96,2048]{2,1,0:T(8,128)(2,1)} async-done(((bf16[16,96,1024]{2,1,0:T(8,128)(2,1)}), bf16[16,96,2048]{2,1,0:T(8,128)(2,1)}) %all-gather.2.cloned.1.call-update) | async-done | bytes 6291472 | tf_op jit(solution)/shard_map/all_gather | solution.py:125
  336.3 6.1 %fusion.10 = f32[1536,384]{1,0:T(8,128)S(1)} fusion(bf16[1536,2048]{1,0:T(8,128)(2,1)} %bitcast.100, bf16[1,2048,384]{2,1,0:T(8,128)(2,1)} %param.17), kind=kOutput, calls=%fused_computation.19 | convolution fusion | flops 2415919104 | bytes 10223616 | tf_op jit(solution)/shard_map/dot_general | solution.py:127
  342.5 3.9 fusion.4
  346.4 5.4 %convolution_convert_fusion = bf16[16,96,2048]{2,1,0:T(8,128)(2,1)} fusion(bf16[16,96,384]{2,1,0:T(8,128)(2,1)S(1)} %bitcast.102, bf16[1,384,2048]{2,1,0:T(8,128)(2,1)S(1)} %copy-done), kind=kOutput, calls=%fused_computation.3 | convolution fusion | flops 2419064832 | bytes 9043968 | tf_op jit(solution)/shard_map/dot_general | solution.py:130
  351.8 77.3 %reduce-scatter.5.cloned.1.call-done = bf16[16,96,1024]{2,1,0:T(8,128)(2,1)} async-done(((bf16[16,96,2048]{2,1,0:T(8,128)(2,1)}), bf16[16,96,1024]{2,1,0:T(8,128)(2,1)}) %reduce-scatter.5.cloned.1.call-update) | async-done | bytes 3145744 | tf_op jit(solution)/shard_map/reduce_scatter | solution.py:134
  429.1 5.6 %all-to-all-start.1 = ((bf16[16,96,1024]{2,1,0:T(8,128)(2,1)}), bf16[16,96,1024]{2,1,0:T(8,128)(2,1)}, u32[]{:S(2)}, u32[]{:S(2)}) async-start(bf16[16,96,1024]{2,1,0:T(8,128)(2,1)} %reduce-scatter.5.cloned.1.call-done), calls=%async_computation.3 | async-start | bytes 6291456 | tf_op jit(solution)/shard_map/all_to_all | solution.py:133
  434.9 72.2 %all-to-all-done.1 = bf16[16,96,1024]{2,1,0:T(8,128)(2,1)} async-done(((bf16[16,96,1024]{2,1,0:T(8,128)(2,1)}), bf16[16,96,1024]{2,1,0:T(8,128)(2,1)}, u32[]{:S(2)}, u32[]{:S(2)}) %all-to-all-start.1) | async-done | bytes 3145760 | tf_op jit(solution)/shard_map/all_to_all | solution.py:133
  507.0 8.4 %gather_fusion.1 = bf16[1024,1024]{1,0:T(8,128)(2,1)} fusion(bf16[1536,1024]{1,0:T(8,128)(2,1)} %bitcast.21, s32[1024]{0:T(1024)S(1)} %broadcast_clamp_fusion), kind=kCustom, calls=%fused_computation.1 | custom fusion | bytes 4198400 | tf_op jit(solution)/shard_map/gather | solution.py:143
  515.4 2.9 fusion
  (61 shorter events, 8.5 us)
Async XLA Ops:
  6.5 339.8 %copy-start = (bf16[1,384,2048]{2,1,0:T(8,128)(2,1)S(1)}, bf16[1,384,2048]{2,1,0:T(8,128)(2,1)}, u32[]{:S(2)}) copy-start(bf16[1,384,2048]{2,1,0:T(8,128)(2,1)} %param.19) | copy-start | bytes 4718596
  6.5 17.7 %copy-start.6 = (s32[1,128,8]{1,2,0:T(8,128)S(1)}, s32[1,128,8]{1,2,0:T(8,128)}, u32[]{:S(2)}) copy-start(s32[1,128,8]{1,2,0:T(8,128)} %param.20) | copy-start | bytes 12292
  6.5 51.8 %copy-start.5 = (bf16[1,128,256]{2,1,0:T(8,128)(2,1)S(1)}, bf16[1,128,256]{2,1,0:T(8,128)(2,1)}, u32[]{:S(2)}) copy-start(bf16[1,128,256]{2,1,0:T(8,128)(2,1)} %param.13) | copy-start | bytes 196612
  6.5 159.2 %reduce-scatter.3.cloned.1.call-start = ((), (), s32[]{:S(2)}) async-start(), calls=%async_computation.4 | async-start | bytes 786432 | tf_op jit(solution)/shard_map/reduce_scatter | solution.py:91
  6.5 50.8 %collective-permute-start = (bf16[2048,512]{1,0:T(8,128)(2,1)}, bf16[2048,512]{1,0:T(8,128)(2,1)}, u32[]{:S(2)}, u32[]{:S(2)}) collective-permute-start(bf16[2048,512]{1,0:T(8,128)(2,1)} %param.15), channel_id=1, source_target_pairs={{0,2},{2,4},{4,6},{6,0},{1,3},{3,5},{5,7},{7,1},{8,10},{10,12},{12... | collective-permute-start | bytes 6291464 | tf_op jit(solution)/shard_map/ppermute | solution.py:20
  9.6 93.2 %collective-permute-start.1 = (bf16[2048,512]{1,0:T(8,128)(2,1)}, bf16[2048,512]{1,0:T(8,128)(2,1)}, u32[]{:S(2)}, u32[]{:S(2)}) collective-permute-start(bf16[2048,512]{1,0:T(8,128)(2,1)} %param.15), channel_id=1, source_target_pairs={{0,6},{2,0},{4,2},{6,4},{1,7},{3,1},{5,3},{7,5},{8,14},{10,8},{12,... | collective-permute-start | bytes 6291464 | tf_op jit(solution)/shard_map/ppermute | solution.py:25
  57.3 89.0 %collective-permute-start.2 = (bf16[2048,512]{1,0:T(8,128)(2,1)}, bf16[2048,512]{1,0:T(8,128)(2,1)}, u32[]{:S(2)}, u32[]{:S(2)}) collective-permute-start(bf16[2048,512]{1,0:T(8,128)(2,1)} %collective-permute-done), channel_id=1, source_target_pairs={{0,2},{2,4},{4,6},{6,0},{1,3},{3,5},{5,7},{7,1},{8,10},{10,12},{12... | collective-permute-start | bytes 6291464 | tf_op jit(solution)/shard_map/ppermute | solution.py:20
  71.8 1.6 copy-start.3
  73.4 2.2 copy-start.1
  148.3 17.5 %copy-start.4 = (bf16[1,128,2048]{2,1,0:T(8,128)(2,1)S(1)}, bf16[1,128,2048]{2,1,0:T(8,128)(2,1)}, u32[]{:S(2)}) copy-start(bf16[1,128,2048]{2,1,0:T(8,128)(2,1)} %param.14) | copy-start | bytes 1572868
  148.3 23.5 %copy-start.7 = (f32[1024]{0:T(1024)S(1)}, f32[1024]{0:T(1024)}, u32[]{:S(2)}) copy-start(f32[1024]{0:T(1024)} %param.16) | copy-start | bytes 12292
  150.4 185.9 %all-gather.2.cloned.1.call-start = ((), (), s32[]{:S(2)}) async-start(), calls=%async_computation.5 | async-start | bytes 9437184 | tf_op jit(solution)/shard_map/all_gather | solution.py:125
  258.6 170.5 %reduce-scatter.5.cloned.1.call-start = ((), (), s32[]{:S(2)}) async-start(), calls=%async_computation.6 | async-start | bytes 9437184 | tf_op jit(solution)/shard_map/reduce_scatter | solution.py:134
  336.3 6.1 %copy-start.9 = (bf16[16,96,2048]{2,1,0:T(8,128)(2,1)S(1)}, bf16[16,96,2048]{2,1,0:T(8,128)(2,1)}, u32[]{:S(2)}) copy-start(bf16[16,96,2048]{2,1,0:T(8,128)(2,1)} %all-gather.2.cloned.1.call-done) | copy-start | bytes 18874372
  336.3 6.1 %copy-start.10 = (bf16[1,2048,384]{2,1,0:T(8,128)(2,1)S(1)}, bf16[1,2048,384]{2,1,0:T(8,128)(2,1)}, u32[]{:S(2)}) copy-start(bf16[1,2048,384]{2,1,0:T(8,128)(2,1)} %param.18) | copy-start | bytes 4718596
  351.8 83.0 %copy-start.8 = (f32[1,128,8]{1,2,0:T(8,128)S(1)}, f32[1,128,8]{1,2,0:T(8,128)}, u32[]{:S(2)}) copy-start(f32[1,128,8]{1,2,0:T(8,128)} %param.21) | copy-start | bytes 12292
  429.1 77.9 %all-to-all-start.1 = ((bf16[16,96,1024]{2,1,0:T(8,128)(2,1)}), bf16[16,96,1024]{2,1,0:T(8,128)(2,1)}, u32[]{:S(2)}, u32[]{:S(2)}) async-start(bf16[16,96,1024]{2,1,0:T(8,128)(2,1)} %reduce-scatter.5.cloned.1.call-done), calls=%async_computation.3 | async-start | bytes 6291456 | tf_op jit(solution)/shard_map/all_to_all | solution.py:133
  507.0 11.3 %copy-start.2 = (bf16[128,1024]{1,0:T(8,128)(2,1)S(1)}, bf16[128,1024]{1,0:T(8,128)(2,1)}, u32[]{:S(2)}) copy-start(bf16[128,1024]{1,0:T(8,128)(2,1)} %reduce-scatter.3.cloned.1.call-done) | copy-start | bytes 786436
Sparse Core Ops, SparseCore 0:
  150.5 15.1 reduce-scatter.2
  258.7 77.5 all-gather.1
  351.9 77.1 reduce-scatter.4
